TPU v7x, 128 devices: a whole 4x4x4 slice. The times are simulated.
128 devices in a mesh: expert: 32 (over y, x_hi, z), tensor: 4 (over x_lo, core).
Axes of the slice: x: 4 (x_hi: 2, x_lo: 2; x = x_hi * 2 + x_lo), y: 4, z: 4, core: 2. Of those that a mesh axis runs over, the one named last changes fastest.
Arguments:
- hidden_in: bfloat16 [16384, 4096], P(('expert', 'tensor')), may hold values from -20 to 20
- context: bfloat16 [16384, 4096], P('expert', 'tensor'), may hold values from -6 to 6
- w_out: bfloat16 [4096, 4096], P('tensor', 'expert'), may hold values from -0.09375 to 0.09375
- norm_gain: float32 [4096], replicated, may hold values from 0.25 to 1.75
- expert_ids: int32 [16384, 8], P(('expert', 'tensor')), may hold values from 0 to 127, all different within a row; in each aligned block of 128 rows (0 to 127, 128 to 255, ...) at most 9 rows name the same one
- route_weight: float32 [16384, 8], P(('expert', 'tensor')), may hold values from 0.05 to 1
- w_gate_up: bfloat16 [128, 4096, 1536], P(('expert', 'tensor')), may hold values from -0.09375 to 0.09375
- w_down: bfloat16 [128, 768, 4096], P(('expert', 'tensor')), may hold values from -0.21875 to 0.21875
Outputs:
- attended: bfloat16 [16384, 4096], P(('expert', 'tensor'))
- mixed: bfloat16 [16384, 4096], P(('expert', 'tensor'))
Inputs may be any that keep to these rules, and one draw needn't show every extreme that they name: `expert_ids`: each row names 8 different experts. Among the 128 rows of one device no expert is named more than 9 times, and in every draw some expert is named exactly 9 times by the rows of some device.
All inputs are finite; a program needn't handle non-finite values.
Results may differ from a plain program's by a relative error of at most 0.0053.
Values may be sent and summed in bfloat16 or wider, within the bound.
A program may use at most 128 MiB of HBM per device.

v0:
```python
import jax
import jax.numpy as jnp
import numpy as np
from jax import lax
from jax.sharding import Mesh
from jax.sharding import PartitionSpec as P

LANES = 128
ALL = ("expert", "xlo", "core")


def expert_block(received, w_gate_up, w_down):
    hidden_units = w_down.shape[1]
    gate_and_up = jnp.dot(received, w_gate_up[0], preferred_element_type=jnp.float32)
    activated = (jax.nn.silu(gate_and_up[:, :hidden_units]) * gate_and_up[:, hidden_units:]).astype(
        jnp.bfloat16
    )
    return jnp.dot(activated, w_down[0], preferred_element_type=jnp.float32).astype(jnp.bfloat16)


def project(context, w_out):
    n_x = lax.axis_size("xlo")
    n_c = lax.axis_size("core")
    rows = context.shape[0] // (n_x * n_c)
    context = (
        context.reshape(n_x, n_c, rows, -1).transpose(1, 0, 2, 3).reshape(n_x * n_c * rows, -1)
    )
    partial_sums = jnp.dot(
        context,
        lax.all_gather(w_out, "expert", axis=1, tiled=True),
        preferred_element_type=jnp.float32,
    )
    width = partial_sums.shape[1]
    chip_sums = lax.psum_scatter(partial_sums, "core", scatter_dimension=0, tiled=True)
    chip_sums = chip_sums.reshape(n_x, rows, width)
    me = lax.axis_index("xlo")
    own = lax.dynamic_index_in_dim(chip_sums, me, axis=0, keepdims=False)
    other = lax.dynamic_index_in_dim(chip_sums, 1 - me, axis=0, keepdims=False)
    arrived = lax.ppermute(other.astype(jnp.bfloat16), "xlo", perm=[(0, 1), (1, 0)])
    return own + arrived.astype(jnp.float32)


def on_device(hidden_in, context, w_out, norm_gain, expert_ids, route_weight, w_gate_up, w_down):
    tok_count, width = hidden_in.shape
    chunks = width // LANES
    projected = project(context, w_out)
    residual = hidden_in.astype(jnp.float32) + projected
    attended = residual.astype(jnp.bfloat16)
    inverse = lax.rsqrt(jnp.mean(residual * residual, axis=1, keepdims=True) + 1e-06)
    normed = (residual * inverse * norm_gain[None, :]).astype(jnp.bfloat16)
    top_count = expert_ids.shape[1]
    experts_all = lax.axis_size(ALL)
    capacity = tok_count * top_count * 9 // (8 * experts_all)
    rows_all = experts_all * capacity
    chosen = expert_ids.reshape(-1)
    onehot = (chosen[:, None] == jnp.arange(experts_all, dtype=jnp.int32)[None, :]).astype(
        jnp.int32
    )
    before = jnp.cumsum(onehot, axis=0) - onehot
    slots = jnp.sum(before * onehot, axis=1)
    target = chosen * capacity + slots
    token_index = jnp.arange(tok_count * top_count, dtype=jnp.int32) // top_count
    source = jnp.full((rows_all,), tok_count, jnp.int32).at[target].set(token_index)
    normed3 = jnp.concatenate(
        [normed.reshape(tok_count, chunks, LANES), jnp.zeros((1, chunks, LANES), jnp.bfloat16)],
        axis=0,
    )
    send = jnp.take(normed3, source, axis=0)
    send = send.reshape(experts_all, capacity * chunks, LANES)
    received = lax.all_to_all(send, ALL, split_axis=0, concat_axis=0, tiled=True)
    outputs = expert_block(received.reshape(rows_all, width), w_gate_up, w_down)
    outputs = outputs.reshape(experts_all, capacity * chunks, LANES)
    returned = lax.all_to_all(outputs, ALL, split_axis=0, concat_axis=0, tiled=True)
    returned = returned.reshape(rows_all, chunks, LANES)
    picked = jnp.take(returned, target, axis=0).reshape(tok_count, top_count, chunks, LANES)
    moe_sum = jnp.sum(route_weight[:, :, None, None] * picked.astype(jnp.float32), axis=1)
    mixed = (residual + moe_sum.reshape(tok_count, width)).astype(jnp.bfloat16)
    return (attended, mixed)


def solution(mesh):
    n_expert = mesh.shape["expert"]
    n_tensor = mesh.shape["tensor"]
    n_core = 2 if n_tensor % 2 == 0 else 1
    devices = np.asarray(mesh.devices).reshape(n_expert, n_tensor // n_core, n_core)
    mesh3 = Mesh(devices, ALL)
    tensor = ("xlo", "core")
    in_specs = (
        P(ALL, None),
        P("expert", tensor),
        P(tensor, "expert"),
        P(),
        P(ALL, None),
        P(ALL, None),
        P(ALL, None, None),
        P(ALL, None, None),
    )
    out_specs = (P(ALL, None), P(ALL, None))
    return jax.shard_map(
        on_device, mesh=mesh3, in_specs=in_specs, out_specs=out_specs, check_vma=False
    )
```

profile of v0, /device:TPU:54, one launch (start us, length us, event | category | flops | bytes accessed | tf_op | source)
XLA Modules:
  0.0 561.1 jit_solution(10142530440497520180)
XLA Ops:
  7.2 0.0 all-gather.2.cloned.1.call-start
  7.2 0.7 all-gather.2.cloned.1.call-update
  7.9 0.0 reduce-scatter.2.cloned.1.call-start
  7.9 1.3 copy.29
  9.2 131.0 %all-gather.2.cloned.1.call-done = bf16[1024,4096]{1,0:T(8,128)(2,1)} async-done(((bf16[1024,128]{1,0:T(8,128)(2,1)}), bf16[1024,4096]{1,0:T(8,128)(2,1)}) %all-gather.2.cloned.1.call-update) | async-done | bytes 8388624 | tf_op jit(solution)/shard_map/all_gather | solution.py:30
  140.2 10.0 %fusion.22 = f32[512,4096]{1,0:T(8,128)} fusion(bf16[512,1024]{1,0:T(8,128)(2,1)S(1)} %bitcast.54, bf16[1024,4096]{1,0:T(8,128)(2,1)} %all-gather.2.cloned.1.call-done), kind=kOutput, calls=%fused_computation.50 | convolution fusion | flops 4294967296 | bytes 17825792 | tf_op jit(solution)/shard_map/dot_general | solution.py:28
  150.3 0.0 copy-start
  150.3 0.0 reduce-scatter.2.cloned.1.call-update
  150.3 0.0 copy-start.1
  150.3 0.6 copy-done
  151.0 0.1 copy.31
  151.1 0.1 eq.26
  151.2 0.1 copy.33
  151.3 0.2 fusion.12
  151.6 19.2 %reduce-scatter.2.cloned.1.call-done = f32[256,4096]{1,0:T(8,128)} async-done(((f32[512,4096]{1,0:T(8,128)}), f32[256,4096]{1,0:T(8,128)}) %reduce-scatter.2.cloned.1.call-update) | async-done | bytes 4194320 | tf_op jit(solution)/shard_map/reduce_scatter | solution.py:34
  170.8 1.7 fusion.8
  172.5 0.9 collective-permute-start
  173.5 0.1 reshape.112
  173.5 0.1 copy.34
  173.7 0.1 copy.37
  173.8 0.1 mul.60
  173.9 0.4 fusion.11
  174.2 4.3 scatter_custom_fusion
  178.6 0.2 broadcast_in_dim.39
  178.8 0.1 copy.38
  178.9 0.2 copy.39
  179.1 18.9 %collective-permute-done = bf16[128,4096]{1,0:T(8,128)(2,1)} collective-permute-done((bf16[128,4096]{1,0:T(8,128)(2,1)S(1)}, bf16[128,4096]{1,0:T(8,128)(2,1)}, u32[]{:S(2)}, u32[]{:S(2)}) %collective-permute-start) | collective-permute-done | bytes 1048608 | tf_op jit(solution)/shard_map/ppermute | solution.py:39
  198.0 2.7 multiply_reduce_fusion.1
  200.7 0.0 copy-done.1
  200.7 0.3 fusion.9
  201.1 0.2 copy.40
  201.3 0.2 concatenate.3
  201.5 6.1 %gather_fusion = bf16[1152,32,128]{2,1,0:T(8,128)(2,1)} fusion(bf16[129,32,128]{2,1,0:T(8,128)(2,1)S(1)} %concatenate.3, s32[2048]{0:T(1024)S(1)} %pad_clamp_fusion), kind=kCustom, calls=%fused_computation | custom fusion | bytes 18878976 | tf_op jit(solution)/shard_map/jit(_take)/gather | solution.py:68
  207.6 8.9 %bitcast_select_fusion = bf16[128,288,128]{2,1,0:T(8,128)(2,1)S(1)} fusion(pred[128,288]{1,0:T(8,128)(4,1)S(1)} %copy.39, bf16[128,288,128]{2,1,0:T(8,128)(2,1)} %bitcast.48), kind=kLoop, calls=%fused_computation.7 | loop fusion | flops 4718592 | bytes 18911232 | tf_op jit(solution)/shard_map/jit(_take)/select_n | solution.py:68
  216.5 120.5 %all_to_all.10 = bf16[128,288,128]{2,1,0:T(8,128)(2,1)} all-to-all(bf16[128,288,128]{2,1,0:T(8,128)(2,1)S(1)} %bitcast_select_fusion), channel_id=1, replica_groups=mesh['expert'=32,'xlo'=2,'core'=2] {'expert','xlo','core'}, dimensions={0} | all-to-all | bytes 18874368 | tf_op jit(solution)/shard_map/all_to_all | solution.py:70
  337.0 14.8 %reshape.115 = bf16[1152,4096]{1,0:T(8,128)(2,1)} reshape(bf16[128,288,128]{2,1,0:T(8,128)(2,1)} %all_to_all.10) | data formatting | bytes 18874368 | tf_op jit(solution)/shard_map/reshape | solution.py:71
  351.8 18.2 %fusion = f32[1152,1536]{1,0:T(8,128)S(1)} fusion(bf16[1152,4096]{1,0:T(8,128)(2,1)} %reshape.115, bf16[1,4096,1536]{2,1,0:T(8,128)(2,1)} %param.14), kind=kOutput, calls=%fused_computation.5 | convolution fusion | flops 14495514624 | bytes 29097984 | tf_op jit(solution)/shard_map/dot_general | solution.py:14
  370.1 12.5 %convolution_convert_fusion = bf16[1152,4096]{1,0:T(8,128)(2,1)} fusion(bf16[1,768,4096]{2,1,0:T(8,128)(2,1)} %param.15, f32[1152,1536]{1,0:T(8,128)S(1)} %fusion), kind=kOutput, calls=%fused_computation.4 | convolution fusion | flops 7257784320 | bytes 22806528 | tf_op jit(solution)/shard_map/dot_general | solution.py:18
  382.6 15.0 %reshape.116 = bf16[128,288,128]{2,1,0:T(8,128)(2,1)} reshape(bf16[1152,4096]{1,0:T(8,128)(2,1)} %convolution_convert_fusion) | data formatting | bytes 18874368 | tf_op jit(solution)/shard_map/reshape | solution.py:72
  397.6 0.0 copy-start.2
  397.6 10.0 %all-to-all-start.1 = ((bf16[128,288,128]{2,1,0:T(8,128)(2,1)}), bf16[128,288,128]{2,1,0:T(8,128)(2,1)}, u32[]{:S(2)}, u32[]{:S(2)}) async-start(bf16[128,288,128]{2,1,0:T(8,128)(2,1)} %reshape.116), calls=%async_computation.2 | async-start | bytes 18874368 | tf_op jit(solution)/shard_map/all_to_all | solution.py:73
  407.6 0.1 reduce_sum.32
  407.7 0.1 copy.36
  407.9 0.0 copy-done.2
  407.9 0.1 copy.30
  408.0 121.9 %all-to-all-done.1 = bf16[128,288,128]{2,1,0:T(8,128)(2,1)} async-done(((bf16[128,288,128]{2,1,0:T(8,128)(2,1)}), bf16[128,288,128]{2,1,0:T(8,128)(2,1)}, u32[]{:S(2)}, u32[]{:S(2)}) %all-to-all-start.1) | async-done | bytes 9437216 | tf_op jit(solution)/shard_map/all_to_all | solution.py:73
  529.9 13.5 %gather_fusion.1 = bf16[1024,32,128]{2,1,0:T(8,128)(2,1)} fusion(bf16[1152,32,128]{2,1,0:T(8,128)(2,1)} %bitcast.15, s32[1024]{0:T(1024)S(1)} %broadcast_clamp_fusion), kind=kCustom, calls=%fused_computation.1 | custom fusion | bytes 16781312 | tf_op jit(solution)/shard_map/jit(_take)/gather | solution.py:75
  543.4 8.2 %multiply_reduce_fusion = f32[128,32,128]{2,1,0:T(8,128)S(1)} fusion(f32[128,8]{1,0:T(8,128)S(1)} %copy.30, pred[128,8]{1,0:T(8,128)(4,1)S(1)} %copy.36, bf16[1024,32,128]{2,1,0:T(8,128)(2,1)} %gather_fusion.1), kind=kLoop, calls=%fused_computation.3 | loop fusion | flops 16252928 | bytes 10490880 | tf_op jit(solution)/shard_map/reduce_sum | solution.py:76
  551.6 2.6 fusion.4
  (15 shorter events, 0.2 us)
Async XLA Ops:
  7.2 133.1 %all-gather.2.cloned.1.call-start = ((), (), s32[]{:S(2)}) async-start(), calls=%async_computation.3 | async-start | bytes 8650752 | tf_op jit(solution)/shard_map/all_gather | solution.py:30
  7.9 162.9 %reduce-scatter.2.cloned.1.call-start = ((), (), s32[]{:S(2)}) async-start(), calls=%async_computation.4 | async-start | bytes 12582912 | tf_op jit(solution)/shard_map/reduce_scatter | solution.py:34
  150.3 0.7 copy-start
  150.3 50.4 %copy-start.1 = (f32[4096]{0:T(1024)S(1)}, f32[4096]{0:T(1024)}, u32[]{:S(2)}) copy-start(f32[4096]{0:T(1024)} %param.11) | copy-start | bytes 49156
  172.5 25.5 %collective-permute-start = (bf16[128,4096]{1,0:T(8,128)(2,1)S(1)}, bf16[128,4096]{1,0:T(8,128)(2,1)}, u32[]{:S(2)}, u32[]{:S(2)}) collective-permute-start(bf16[128,4096]{1,0:T(8,128)(2,1)S(1)} %fusion.8), channel_id=1, source_target_pairs={{0,2},{2,0},{1,3},{3,1},{4,6},{6,4},{5,7},{7,5},{8,10},{10,8},{9,1... | collective-permute-start | bytes 3145736 | tf_op jit(solution)/shard_map/ppermute | solution.py:39
  397.6 10.3 %copy-start.2 = (f32[128,8]{0,1:T(8,128)S(1)}, f32[128,8]{0,1:T(8,128)}, u32[]{:S(2)}) copy-start(f32[128,8]{0,1:T(8,128)} %param.13) | copy-start | bytes 12292
  397.6 132.3 %all-to-all-start.1 = ((bf16[128,288,128]{2,1,0:T(8,128)(2,1)}), bf16[128,288,128]{2,1,0:T(8,128)(2,1)}, u32[]{:S(2)}, u32[]{:S(2)}) async-start(bf16[128,288,128]{2,1,0:T(8,128)(2,1)} %reshape.116), calls=%async_computation.2 | async-start | bytes 18874368 | tf_op jit(solution)/shard_map/all_to_all | solution.py:73
Sparse Core Ops, SparseCore 0:
  10.7 129.4 all-gather.1
  150.4 20.3 reduce-scatter.1
where the time goes:
time: 562 us; the launch traced here: 561 us
  waiting for transfers between devices  292 us (52%)
  blocking collectives  120 us (21%)
  local copies, waits for them, and re-layouts  59.4 us (11%)
  matrix products  40.8 us (7%)
  other arithmetic  23.4 us (4%)
  between operations  14.3 us (3%)
  starting transfers between devices  11 us (2%)
    all_gather x1, waiting for transfers between devices, project(): lax.all_gather(w_out, 'expert', axis=1, tiled=True)  131 us
    all_to_all x1, waiting for transfers between devices, on_device(): lax.all_to_all(outputs, ALL, split_axis=0, concat_axis=0, tiled=True)  122 us
    all_to_all x1, blocking collectives, on_device(): lax.all_to_all(send, ALL, split_axis=0, concat_axis=0, tiled=True)  120 us
    reduce_scatter x1, waiting for transfers between devices, project(): lax.psum_scatter(partial_sums, 'core', scatter_dimension=0, tiled=True)  19.2 us
    ppermute x1, waiting for transfers between devices, project(): lax.ppermute(other.astype(jnp.bfloat16), 'xlo', perm=[(0, 1), (1, 0)])  18.9 us
    dot_general x1, matrix products, expert_block(): jnp.dot(received, w_gate_up[0], preferred_element_type=jnp.float32)  18.2 us
    reshape x1, local copies, waits for them, and re-layouts, on_device(): outputs = outputs.reshape(experts_all, capacity * chunks, LANES)  15 us
    reshape x1, local copies, waits for them, and re-layouts, on_device(): outputs = expert_block(received.reshape(rows_all, width), w_gate_up, w_down)  14.8 us
  transfers between devices with their start and end apart: 4, of which 4 were waited for; matrix products, arithmetic and copies ran while one was open for 1% of the time, Pallas kernels for 0%

commit v1 on v0

--- a/solution.py
+++ b/solution.py
@@ -27,7 +27,9 @@
     )
     partial_sums = jnp.dot(
         context,
-        lax.all_gather(w_out, "expert", axis=1, tiled=True),
+        jnp.concatenate(
+            lax.all_to_all(jnp.stack([w_out] * lax.axis_size("expert")), "expert", 0, 0), axis=1
+        ),
         preferred_element_type=jnp.float32,
     )
     width = partial_sums.shape[1]

time: 562 us -> 583 us (1.037)
  starting transfers between devices: 11 us -> 21.5 us
    all_gather x1 -> x0, waiting for transfers between devices: 131 us -> none  [project(): lax.all_gather(w_out, 'expert', axis=1, tiled=True)]
    all_to_all x0 -> x1, waiting for transfers between devices: none -> 123 us  [project(): lax.all_to_all(jnp.stack([w_out] * lax.axis_size('expert')), 'expert', 0, 0)]
    reduce_scatter x1, waiting for transfers between devices: 19.2 us -> 33.1 us  [project(): lax.psum_scatter(partial_sums, 'core', scatter_dimension=0, tiled=True)]
    all_to_all x0 -> x1, starting transfers between devices: none -> 10.6 us  [project(): lax.all_to_all(jnp.stack([w_out] * lax.axis_size('expert')), 'expert', 0, 0)]
where the time goes in v1:
time: 583 us; the launch traced here: 581 us
  waiting for transfers between devices  297 us (51%)
  blocking collectives  121 us (21%)
  local copies, waits for them, and re-layouts  63.6 us (11%)
  matrix products  40.8 us (7%)
  other arithmetic  23.4 us (4%)
  starting transfers between devices  21.5 us (4%)
  between operations  14.3 us (2%)
    all_to_all x1, waiting for transfers between devices, project(): lax.all_to_all(jnp.stack([w_out] * lax.axis_size('expert')), 'expert', 0, 0)  123 us
    all_to_all x1, waiting for transfers between devices, on_device(): lax.all_to_all(outputs, ALL, split_axis=0, concat_axis=0, tiled=True)  122 us
    all_to_all x1, blocking collectives, on_device(): lax.all_to_all(send, ALL, split_axis=0, concat_axis=0, tiled=True)  121 us
    reduce_scatter x1, waiting for transfers between devices, project(): lax.psum_scatter(partial_sums, 'core', scatter_dimension=0, tiled=True)  33.1 us
    ppermute x1, waiting for transfers between devices, project(): lax.ppermute(other.astype(jnp.bfloat16), 'xlo', perm=[(0, 1), (1, 0)])  18.8 us
    dot_general x1, matrix products, expert_block(): jnp.dot(received, w_gate_up[0], preferred_element_type=jnp.float32)  18.2 us
    reshape x1, local copies, waits for them, and re-layouts, on_device(): outputs = outputs.reshape(experts_all, capacity * chunks, LANES)  15 us
    reshape x1, local copies, waits for them, and re-layouts, on_device(): outputs = expert_block(received.reshape(rows_all, width), w_gate_up, w_down)  14.8 us
  transfers between devices with their start and end apart: 4, of which 4 were waited for; matrix products, arithmetic and copies ran while one was open for 1% of the time, Pallas kernels for 0%

profile of v1, /device:TPU:54, one launch (start us, length us, event | category | flops | bytes accessed | tf_op | source)
XLA Modules:
  0.0 581.5 jit_solution(17636422822209441736)
XLA Ops:
  7.2 1.1 copy.32
  8.3 4.3 stack.2
  12.5 0.0 copy-start
  12.5 10.6 %all-to-all-start = ((bf16[32,1024,128]{1,2,0:T(8,128)(2,1)}), bf16[32,1024,128]{1,2,0:T(8,128)(2,1)}, u32[]{:S(2)}, u32[]{:S(2)}) async-start(bf16[32,1024,128]{1,2,0:T(8,128)(2,1)} %stack.2), calls=%async_computation | async-start | bytes 16777216 | tf_op jit(solution)/shard_map/all_to_all | solution.py:31
  23.1 0.0 reduce-scatter.2.cloned.1.call-start
  23.2 0.0 copy-done
  23.2 0.1 copy.31
  23.3 123.5 %all-to-all-done = bf16[32,1024,128]{1,2,0:T(8,128)(2,1)} async-done(((bf16[32,1024,128]{1,2,0:T(8,128)(2,1)}), bf16[32,1024,128]{1,2,0:T(8,128)(2,1)}, u32[]{:S(2)}, u32[]{:S(2)}) %all-to-all-start) | async-done | bytes 8388640 | tf_op jit(solution)/shard_map/all_to_all | solution.py:31
  146.8 10.1 %fusion.22 = f32[512,4096]{1,0:T(8,128)} fusion(bf16[512,1024]{1,0:T(8,128)(2,1)S(1)} %bitcast.57, bf16[1024,4096]{0,1:T(8,128)(2,1)} %bitcast.4), kind=kOutput, calls=%fused_computation.50 | convolution fusion | flops 4294967296 | bytes 17825792 | tf_op jit(solution)/shard_map/dot_general | solution.py:28
  156.9 0.0 copy-start.1
  156.9 0.0 reduce-scatter.2.cloned.1.call-update
  156.9 0.0 copy-start.2
  156.9 0.6 copy-done.1
  157.6 0.1 copy.34
  157.7 0.1 eq.26
  157.7 0.1 copy.36
  157.9 0.2 fusion.12
  158.1 33.1 %reduce-scatter.2.cloned.1.call-done = f32[256,4096]{1,0:T(8,128)} async-done(((f32[512,4096]{1,0:T(8,128)}), f32[256,4096]{1,0:T(8,128)}) %reduce-scatter.2.cloned.1.call-update) | async-done | bytes 4194320 | tf_op jit(solution)/shard_map/reduce_scatter | solution.py:36
  191.2 1.7 fusion.8
  192.9 0.9 collective-permute-start
  193.9 0.1 reshape.122
  194.0 0.1 copy.37
  194.1 0.1 copy.40
  194.2 0.1 mul.60
  194.3 0.4 fusion.11
  194.7 4.3 scatter_custom_fusion
  199.0 0.2 broadcast_in_dim.39
  199.3 0.1 copy.41
  199.4 0.2 copy.42
  199.6 18.8 %collective-permute-done = bf16[128,4096]{1,0:T(8,128)(2,1)} collective-permute-done((bf16[128,4096]{1,0:T(8,128)(2,1)S(1)}, bf16[128,4096]{1,0:T(8,128)(2,1)}, u32[]{:S(2)}, u32[]{:S(2)}) %collective-permute-start) | collective-permute-done | bytes 1048608 | tf_op jit(solution)/shard_map/ppermute | solution.py:41
  218.4 2.7 multiply_reduce_fusion.1
  221.1 0.0 copy-done.2
  221.1 0.3 fusion.9
  221.5 0.2 copy.43
  221.7 0.2 concatenate.3
  221.9 6.1 %gather_fusion = bf16[1152,32,128]{2,1,0:T(8,128)(2,1)} fusion(bf16[129,32,128]{2,1,0:T(8,128)(2,1)S(1)} %concatenate.3, s32[2048]{0:T(1024)S(1)} %pad_clamp_fusion), kind=kCustom, calls=%fused_computation | custom fusion | bytes 18878976 | tf_op jit(solution)/shard_map/jit(_take)/gather | solution.py:70
  228.0 8.9 %bitcast_select_fusion = bf16[128,288,128]{2,1,0:T(8,128)(2,1)S(1)} fusion(pred[128,288]{1,0:T(8,128)(4,1)S(1)} %copy.42, bf16[128,288,128]{2,1,0:T(8,128)(2,1)} %bitcast.51), kind=kLoop, calls=%fused_computation.7 | loop fusion | flops 4718592 | bytes 18911232 | tf_op jit(solution)/shard_map/jit(_take)/select_n | solution.py:70
  236.9 120.5 %all_to_all.15 = bf16[128,288,128]{2,1,0:T(8,128)(2,1)} all-to-all(bf16[128,288,128]{2,1,0:T(8,128)(2,1)S(1)} %bitcast_select_fusion), channel_id=1, replica_groups=mesh['expert'=32,'xlo'=2,'core'=2] {'expert','xlo','core'}, dimensions={0} | all-to-all | bytes 18874368 | tf_op jit(solution)/shard_map/all_to_all | solution.py:72
  357.4 14.8 %reshape.125 = bf16[1152,4096]{1,0:T(8,128)(2,1)} reshape(bf16[128,288,128]{2,1,0:T(8,128)(2,1)} %all_to_all.15) | data formatting | bytes 18874368 | tf_op jit(solution)/shard_map/reshape | solution.py:73
  372.3 18.2 %fusion = f32[1152,1536]{1,0:T(8,128)S(1)} fusion(bf16[1152,4096]{1,0:T(8,128)(2,1)} %reshape.125, bf16[1,4096,1536]{2,1,0:T(8,128)(2,1)} %param.14), kind=kOutput, calls=%fused_computation.5 | convolution fusion | flops 14495514624 | bytes 29097984 | tf_op jit(solution)/shard_map/dot_general | solution.py:14
  390.5 12.5 %convolution_convert_fusion = bf16[1152,4096]{1,0:T(8,128)(2,1)} fusion(bf16[1,768,4096]{2,1,0:T(8,128)(2,1)} %param.15, f32[1152,1536]{1,0:T(8,128)S(1)} %fusion), kind=kOutput, calls=%fused_computation.4 | convolution fusion | flops 7257784320 | bytes 22806528 | tf_op jit(solution)/shard_map/dot_general | solution.py:18
  403.0 15.0 %reshape.126 = bf16[128,288,128]{2,1,0:T(8,128)(2,1)} reshape(bf16[1152,4096]{1,0:T(8,128)(2,1)} %convolution_convert_fusion) | data formatting | bytes 18874368 | tf_op jit(solution)/shard_map/reshape | solution.py:74
  418.0 0.0 copy-start.3
  418.0 10.0 %all-to-all-start.2 = ((bf16[128,288,128]{2,1,0:T(8,128)(2,1)}), bf16[128,288,128]{2,1,0:T(8,128)(2,1)}, u32[]{:S(2)}, u32[]{:S(2)}) async-start(bf16[128,288,128]{2,1,0:T(8,128)(2,1)} %reshape.126), calls=%async_computation.3 | async-start | bytes 18874368 | tf_op jit(solution)/shard_map/all_to_all | solution.py:75
  428.0 0.1 reduce_sum.32
  428.1 0.1 copy.39
  428.3 0.0 copy-done.3
  428.3 0.1 copy.33
  428.4 121.9 %all-to-all-done.2 = bf16[128,288,128]{2,1,0:T(8,128)(2,1)} async-done(((bf16[128,288,128]{2,1,0:T(8,128)(2,1)}), bf16[128,288,128]{2,1,0:T(8,128)(2,1)}, u32[]{:S(2)}, u32[]{:S(2)}) %all-to-all-start.2) | async-done | bytes 9437216 | tf_op jit(solution)/shard_map/all_to_all | solution.py:75
  550.3 13.5 %gather_fusion.1 = bf16[1024,32,128]{2,1,0:T(8,128)(2,1)} fusion(bf16[1152,32,128]{2,1,0:T(8,128)(2,1)} %bitcast.17, s32[1024]{0:T(1024)S(1)} %broadcast_clamp_fusion), kind=kCustom, calls=%fused_computation.1 | custom fusion | bytes 16781312 | tf_op jit(solution)/shard_map/jit(_take)/gather | solution.py:77
  563.8 8.2 %multiply_reduce_fusion = f32[128,32,128]{2,1,0:T(8,128)S(1)} fusion(f32[128,8]{1,0:T(8,128)S(1)} %copy.33, pred[128,8]{1,0:T(8,128)(4,1)S(1)} %copy.39, bf16[1024,32,128]{2,1,0:T(8,128)(2,1)} %gather_fusion.1), kind=kLoop, calls=%fused_computation.3 | loop fusion | flops 16252928 | bytes 10490880 | tf_op jit(solution)/shard_map/reduce_sum | solution.py:78
  572.0 2.6 fusion.4
  (15 shorter events, 0.2 us)
Async XLA Ops:
  12.5 10.7 %copy-start = (bf16[512,1024]{1,0:T(8,128)(2,1)S(1)}, bf16[512,1024]{1,0:T(8,128)(2,1)}, u32[]{:S(2)}) copy-start(bf16[512,1024]{1,0:T(8,128)(2,1)} %param.9) | copy-start | bytes 3145732
  12.5 134.2 %all-to-all-start = ((bf16[32,1024,128]{1,2,0:T(8,128)(2,1)}), bf16[32,1024,128]{1,2,0:T(8,128)(2,1)}, u32[]{:S(2)}, u32[]{:S(2)}) async-start(bf16[32,1024,128]{1,2,0:T(8,128)(2,1)} %stack.2), calls=%async_computation | async-start | bytes 16777216 | tf_op jit(solution)/shard_map/all_to_all | solution.py:31
  23.1 168.1 %reduce-scatter.2.cloned.1.call-start = ((), (), s32[]{:S(2)}) async-start(), calls=%async_computation.4 | async-start | bytes 12582912 | tf_op jit(solution)/shard_map/reduce_scatter | solution.py:36
  156.9 0.7 copy-start.1
  156.9 64.2 %copy-start.2 = (f32[4096]{0:T(1024)S(1)}, f32[4096]{0:T(1024)}, u32[]{:S(2)}) copy-start(f32[4096]{0:T(1024)} %param.11) | copy-start | bytes 49156
  192.9 25.5 %collective-permute-start = (bf16[128,4096]{1,0:T(8,128)(2,1)S(1)}, bf16[128,4096]{1,0:T(8,128)(2,1)}, u32[]{:S(2)}, u32[]{:S(2)}) collective-permute-start(bf16[128,4096]{1,0:T(8,128)(2,1)S(1)} %fusion.8), channel_id=1, source_target_pairs={{0,2},{2,0},{1,3},{3,1},{4,6},{6,4},{5,7},{7,5},{8,10},{10,8},{9,1... | collective-permute-start | bytes 3145736 | tf_op jit(solution)/shard_map/ppermute | solution.py:41
  418.0 10.3 %copy-start.3 = (f32[128,8]{0,1:T(8,128)S(1)}, f32[128,8]{0,1:T(8,128)}, u32[]{:S(2)}) copy-start(f32[128,8]{0,1:T(8,128)} %param.13) | copy-start | bytes 12292
  418.0 132.3 %all-to-all-start.2 = ((bf16[128,288,128]{2,1,0:T(8,128)(2,1)}), bf16[128,288,128]{2,1,0:T(8,128)(2,1)}, u32[]{:S(2)}, u32[]{:S(2)}) async-start(bf16[128,288,128]{2,1,0:T(8,128)(2,1)} %reshape.126), calls=%async_computation.3 | async-start | bytes 18874368 | tf_op jit(solution)/shard_map/all_to_all | solution.py:75
Sparse Core Ops, SparseCore 0:
  157.0 34.1 reduce-scatter.1
